TPU v7x, 512 devices: a whole 4x4x16 slice. The times are simulated.
512 devices in a mesh: dp: 8 (over x, core), expert: 64 (over y, z).
Axes of the slice: x: 4, y: 4, z: 16, core: 2. Of those that a mesh axis runs over, the one named last changes fastest.
Arguments:
- tokens: bfloat16 [8192, 2048], P('expert', 'dp'), may hold values from -6 to 6
- cotangent: bfloat16 [8192, 2048], P('expert', 'dp'), may hold values from -6 to 6
- routes: int32 [8192, 8], P('expert'), may hold values from 0 to 63, as said below
- mix_weights: float32 [8192, 8], P('expert'), may hold values from 0.05 to 0.5
- w_gate: bfloat16 [64, 2048, 384], P('expert', 'dp'), may hold values from -0.125 to 0.125
- w_up: bfloat16 [64, 2048, 384], P('expert', 'dp'), may hold values from -0.125 to 0.125
- w_down: bfloat16 [64, 384, 2048], P('expert', None, 'dp'), may hold values from -0.3125 to 0.3125
Outputs:
- mixed: bfloat16 [8192, 2048], P('expert', 'dp')
- token_grad: bfloat16 [8192, 2048], P('expert', 'dp')
- gate_grad: float32 [64, 2048, 384], P('expert', 'dp')
- up_grad: float32 [64, 2048, 384], P('expert', 'dp')
- down_grad: float32 [64, 384, 2048], P('expert', None, 'dp')
Inputs may be any that keep to these rules, and one draw needn't show every extreme that they name: `routes`: each row names 8 different experts. In each aligned block of 128 rows at most 32 rows name the same expert, and some block reaches that. In all, at most 1792 rows name one expert, and some expert is named by exactly that many.
All inputs are finite; a program needn't handle non-finite values.
Results may differ from a plain program's by a relative error of at most 0.023.
Values may be sent and summed in bfloat16 or wider, within the bound.
A program may use at most 64 MiB of HBM per device.

v0:
```python
import jax
import jax.numpy as jnp
from jax import lax
from jax.sharding import PartitionSpec as P


def contract(left_side, right_side, left_dim, right_dim):
    return lax.dot_general(
        left_side,
        right_side,
        (((left_dim,), (right_dim,)), ((), ())),
        preferred_element_type=jnp.float32,
    )


def silu_parts(gate_in):
    logistic = jax.nn.sigmoid(gate_in)
    return (gate_in * logistic, logistic * (1.0 + gate_in * (1.0 - logistic)))


def shards(tokens, cotangent, routes, mix_weights, w_gate, w_up, w_down):
    tok_rows, width_dev = tokens.shape
    picks_per = routes.shape[1]
    owner_count = lax.axis_size("expert")
    send_cap = 2 * tok_rows * picks_per // owner_count
    expert_cap = 7 * tok_rows * picks_per // 4
    slot_total = owner_count * send_cap
    gate_matrix = w_gate[0]
    up_matrix = w_up[0]
    down_matrix = w_down[0]
    flat_routes = routes.reshape(-1)
    owner_ids = jnp.arange(owner_count, dtype=jnp.int32)
    onehot = (owner_ids[:, None] == flat_routes[None, :]).astype(jnp.int32)
    earlier = jnp.cumsum(onehot, axis=1) - onehot
    rank_in = jnp.sum(earlier * onehot, axis=0)
    slot_index = flat_routes * send_cap + rank_in
    sent_counts = jnp.sum(onehot, axis=1).reshape(owner_count, 1)

    def to_slots(values):
        empty_rows = jnp.zeros((slot_total, width_dev), values.dtype)
        return empty_rows.at[slot_index].set(values).reshape(owner_count, send_cap, width_dev)

    x_slots = to_slots(jnp.repeat(tokens, picks_per, axis=0))
    scaled = mix_weights[:, :, None] * cotangent[:, None, :].astype(jnp.float32)
    grad_slots = to_slots(scaled.astype(jnp.bfloat16).reshape(tok_rows * picks_per, width_dev))
    got_tokens, got_counts = (
        lax.all_to_all(x_slots, "expert", split_axis=0, concat_axis=0, tiled=True),
        lax.all_to_all(sent_counts, "expert", split_axis=0, concat_axis=0, tiled=True),
    )
    counts = got_counts[:, 0]
    starts = jnp.cumsum(counts) - counts
    position = jnp.arange(send_cap, dtype=jnp.int32)
    target = jnp.where(
        position[None, :] < counts[:, None], starts[:, None] + position[None, :], expert_cap
    ).reshape(-1)
    fetch_row = jnp.minimum(target, expert_cap - 1)

    def pack_rows(slot_rows):
        empty_rows = jnp.zeros((expert_cap, width_dev), slot_rows.dtype)
        return empty_rows.at[target].set(slot_rows.reshape(slot_total, width_dev), mode="drop")

    def unpack(rows_in):
        return rows_in[fetch_row].reshape(owner_count, send_cap, width_dev)

    packed_x = pack_rows(got_tokens)
    gate_part = jnp.dot(packed_x, gate_matrix, preferred_element_type=jnp.float32)
    up_part = jnp.dot(packed_x, up_matrix, preferred_element_type=jnp.float32)
    gate_in, up_in = (
        lax.psum(gate_part.astype(jnp.bfloat16), "dp").astype(jnp.float32),
        lax.psum(up_part.astype(jnp.bfloat16), "dp").astype(jnp.float32),
    )
    activated, slope_silu = silu_parts(gate_in)
    hidden_act = (activated * up_in).astype(jnp.bfloat16)
    expert_out = jnp.dot(hidden_act, down_matrix, preferred_element_type=jnp.float32).astype(
        jnp.bfloat16
    )
    back_out = lax.all_to_all(unpack(expert_out), "expert", split_axis=0, concat_axis=0, tiled=True)
    got_grad = lax.all_to_all(grad_slots, "expert", split_axis=0, concat_axis=0, tiled=True)
    packed_grad = pack_rows(got_grad)
    back_hidden = lax.psum(
        contract(packed_grad, down_matrix, 1, 1).astype(jnp.bfloat16), "dp"
    ).astype(jnp.float32)
    gate_back = (back_hidden * up_in * slope_silu).astype(jnp.bfloat16)
    up_back = (back_hidden * activated).astype(jnp.bfloat16)
    row_grad = (contract(gate_back, gate_matrix, 1, 1) + contract(up_back, up_matrix, 1, 1)).astype(
        jnp.bfloat16
    )
    gate_grad = contract(packed_x, gate_back, 0, 0)
    up_grad = contract(packed_x, up_back, 0, 0)
    down_grad = contract(hidden_act, packed_grad, 0, 0)
    back_grad = lax.all_to_all(unpack(row_grad), "expert", split_axis=0, concat_axis=0, tiled=True)

    def collect(returned):
        picked = returned.reshape(slot_total, width_dev)[slot_index]
        return picked.reshape(tok_rows, picks_per, width_dev).astype(jnp.float32)

    mixed = jnp.sum(mix_weights[:, :, None] * collect(back_out), axis=1).astype(jnp.bfloat16)
    token_grad = jnp.sum(collect(back_grad), axis=1).astype(jnp.bfloat16)
    return (mixed, token_grad, gate_grad[None], up_grad[None], down_grad[None])


def solution(mesh):
    placed = (
        P("expert", "dp"),
        P("expert", "dp"),
        P("expert", None),
        P("expert", None),
        P("expert", "dp", None),
        P("expert", "dp", None),
        P("expert", None, "dp"),
    )
    return jax.shard_map(
        shards,
        mesh=mesh,
        in_specs=placed,
        out_specs=(
            P("expert", "dp"),
            P("expert", "dp"),
            P("expert", "dp", None),
            P("expert", "dp", None),
            P("expert", None, "dp"),
        ),
        check_vma=False,
    )
```

profile of v0, /device:TPU:6, one launch (start us, length us, event | category | flops | bytes accessed | tf_op | source)
XLA Modules:
  0.0 434.1 jit_solution(10336787646805802478)
XLA Ops:
  7.2 0.8 copy.41
  8.3 0.7 copy.42
  9.0 18.7 %all-to-all-start = ((s32[64,1,1]{2,1,0:T(1,128)}), s32[64,1,1]{2,1,0:T(1,128)S(1)}, u32[]{:S(2)}, u32[]{:S(2)}) async-start(s32[64,1,1]{2,1,0:T(1,128)} %copy.42), calls=%async_computation | async-start | bytes 65536 | tf_op jit(solution)/shard_map/all_to_all | solution.py:48
  28.7 18.0 %reduce-window.19 = s32[64,8,128]{2,1,0:T(8,128)S(1)} reduce-window(s32[64,8,128]{2,1,0:T(8,128)S(1)} %fusion.25, s32[]{:T(128)} %constant.9.clone.1), window={size=1x1x128 pad=0_0x0_0x127_0}, to_apply=%region_2.3 | reduce-window | flops 8323072 | bytes 524292 | tf_op jit(solution)/shard_map/reduce-window.1
  47.6 6.5 %scatter_custom_fusion.2 = bf16[2048,256]{1,0:T(8,128)(2,1)} fusion(s32[1024]{0:T(1024)S(1)} %bitcast.75, f32[128,256]{1,0:T(8,128)S(1)} %convert_element_type.70, f32[1024]{0:T(1024)S(1)} %mul.74, bf16[]{:T(256)} %constant.8.clone.1), kind=kCustom, calls=%fused_computation.36 | custom fusion | flops 524288 | bytes 1183746 | tf_op jit(solution)/shard_map/scatter | solution.py:41
  54.1 15.1 %all-to-all-start.3 = ((bf16[64,32,256]{2,1,0:T(8,128)(2,1)}), bf16[64,32,256]{2,1,0:T(8,128)(2,1)S(1)}, u32[]{:S(2)}, u32[]{:S(2)}) async-start(bf16[64,32,256]{2,1,0:T(8,128)(2,1)} %bitcast.17), calls=%async_computation.3 | async-start | bytes 2097152 | tf_op jit(solution)/shard_map/all_to_all | solution.py:78
  69.3 6.0 %scatter_custom_fusion = bf16[2048,256]{1,0:T(8,128)(2,1)} fusion(s32[1024]{0:T(1024)S(1)} %bitcast.76, bf16[]{:T(256)} %constant.8.clone.1, bf16[128,256]{1,0:T(8,128)(2,1)S(1)} %copy-done.15), kind=kCustom, calls=%fused_computation.38 | custom fusion | bytes 1114114 | tf_op jit(solution)/shard_map/scatter | solution.py:41
  75.3 47.2 %all-to-all-done.3 = bf16[64,32,256]{2,1,0:T(8,128)(2,1)S(1)} async-done(((bf16[64,32,256]{2,1,0:T(8,128)(2,1)}), bf16[64,32,256]{2,1,0:T(8,128)(2,1)S(1)}, u32[]{:S(2)}, u32[]{:S(2)}) %all-to-all-start.3) | async-done | bytes 1048608 | tf_op jit(solution)/shard_map/all_to_all | solution.py:78
  122.5 6.8 %all-to-all-start.1 = ((bf16[64,32,256]{2,1,0:T(8,128)(2,1)}), bf16[64,32,256]{2,1,0:T(8,128)(2,1)S(1)}, u32[]{:S(2)}, u32[]{:S(2)}) async-start(bf16[64,32,256]{2,1,0:T(8,128)(2,1)} %bitcast.7), calls=%async_computation.1 | async-start | bytes 2097152 | tf_op jit(solution)/shard_map/all_to_all | solution.py:47
  129.8 1.2 reduce.2
  131.2 9.5 %scatter_custom_fusion.3 = bf16[1792,256]{1,0:T(8,128)(2,1)S(1)} fusion(s32[2048]{0:T(1024)S(1)} %bitcast.78, bf16[2048,256]{1,0:T(8,128)(2,1)S(1)} %bitcast.69, bf16[]{:T(256)} %constant.8.clone.1), kind=kCustom, calls=%fused_computation.44 | custom fusion | bytes 917506 | tf_op jit(solution)/shard_map/scatter | solution.py:60
  140.8 42.3 %all-to-all-done.1 = bf16[64,32,256]{2,1,0:T(8,128)(2,1)S(1)} async-done(((bf16[64,32,256]{2,1,0:T(8,128)(2,1)}), bf16[64,32,256]{2,1,0:T(8,128)(2,1)S(1)}, u32[]{:S(2)}, u32[]{:S(2)}) %all-to-all-start.1) | async-done | bytes 1048608 | tf_op jit(solution)/shard_map/all_to_all | solution.py:47
  183.1 9.5 %scatter_custom_fusion.1 = bf16[1792,256]{1,0:T(8,128)(2,1)S(1)} fusion(s32[2048]{0:T(1024)S(1)} %bitcast.79, bf16[2048,256]{1,0:T(8,128)(2,1)S(1)} %bitcast.70, bf16[]{:T(256)} %constant.8.clone.1), kind=kCustom, calls=%fused_computation.46 | custom fusion | bytes 917506 | tf_op jit(solution)/shard_map/scatter | solution.py:60
  192.6 1.7 convolution_convert_fusion.1
  194.3 1.8 convolution_convert_fusion.2
  196.1 1.7 convolution_convert_fusion
  197.9 77.5 %all-reduce.3.cloned.1.call-done = (bf16[1792,384]{1,0:T(8,128)(2,1)}, bf16[1792,384]{1,0:T(8,128)(2,1)}, bf16[1792,384]{1,0:T(8,128)(2,1)}) async-done(((bf16[1792,384]{1,0:T(8,128)(2,1)}, bf16[1792,384]{1,0:T(8,128)(2,1)}, bf16[1792,384]{1,0:T(8,128)(2,1)}), (bf16[1792,384]{1,0:T(8,128)(2,1)}, bf16[1792,384]{1,0:T(8,128)(2,1)}, bf16[1792,384]{1,0:T(8,128)(2,1)})) %all-reduce.3.cloned.1.call-update) | async-done | bytes 4128784 | tf_op jit(solution)/shard_map/psum | solution.py:70
  275.4 3.9 fusion.3
  281.5 9.0 %gather_fusion.2 = bf16[2048,256]{1,0:T(8,128)(2,1)} fusion(bf16[1792,256]{1,0:T(8,128)(2,1)S(1)} %fusion.9, s32[2048]{0:T(1024)S(1)} %broadcast_clamp_fusion), kind=kCustom, calls=%fused_computation.2 | custom fusion | bytes 2105344 | tf_op jit(solution)/shard_map/gather | solution.py:63
  290.4 15.6 %all-to-all-start.4 = ((bf16[64,32,256]{2,1,0:T(8,128)(2,1)}), bf16[64,32,256]{2,1,0:T(8,128)(2,1)S(1)}, u32[]{:S(2)}, u32[]{:S(2)}) async-start(bf16[64,32,256]{2,1,0:T(8,128)(2,1)} %bitcast.68), calls=%async_computation.4 | async-start | bytes 2097152 | tf_op jit(solution)/shard_map/all_to_all | solution.py:91
  306.1 1.6 convolution_convert_fusion.3
  307.7 9.0 %gather_fusion = bf16[2048,256]{1,0:T(8,128)(2,1)} fusion(bf16[1792,256]{1,0:T(8,128)(2,1)S(1)} %convolution_convert_fusion.3, s32[2048]{0:T(1024)S(1)} %broadcast_clamp_fusion), kind=kCustom, calls=%fused_computation | custom fusion | bytes 2105344 | tf_op jit(solution)/shard_map/gather | solution.py:63
  316.6 40.8 %all-to-all-done.4 = bf16[64,32,256]{2,1,0:T(8,128)(2,1)S(1)} async-done(((bf16[64,32,256]{2,1,0:T(8,128)(2,1)}), bf16[64,32,256]{2,1,0:T(8,128)(2,1)S(1)}, u32[]{:S(2)}, u32[]{:S(2)}) %all-to-all-start.4) | async-done | bytes 1048608 | tf_op jit(solution)/shard_map/all_to_all | solution.py:91
  357.4 10.5 %all-to-all-start.2 = ((bf16[64,32,256]{2,1,0:T(8,128)(2,1)}), bf16[64,32,256]{2,1,0:T(8,128)(2,1)S(1)}, u32[]{:S(2)}, u32[]{:S(2)}) async-start(bf16[64,32,256]{2,1,0:T(8,128)(2,1)} %bitcast.67), calls=%async_computation.2 | async-start | bytes 2097152 | tf_op jit(solution)/shard_map/all_to_all | solution.py:77
  368.0 2.9 convolution_bitcast_fusion.1
  370.9 1.4 convolution_bitcast_fusion.2
  372.5 1.3 convolution_bitcast_fusion
  373.8 3.9 gather_fusion.3
  377.7 1.0 bitcast_reduce_fusion
  378.7 43.6 %all-to-all-done.2 = bf16[64,32,256]{2,1,0:T(8,128)(2,1)S(1)} async-done(((bf16[64,32,256]{2,1,0:T(8,128)(2,1)}), bf16[64,32,256]{2,1,0:T(8,128)(2,1)S(1)}, u32[]{:S(2)}, u32[]{:S(2)}) %all-to-all-start.2) | async-done | bytes 1048608 | tf_op jit(solution)/shard_map/all_to_all | solution.py:77
  422.3 3.9 gather_fusion.1
  426.2 1.0 fusion.10
  (64 shorter events, 5.0 us)
Async XLA Ops:
  7.2 187.1 %copy-start = (bf16[1,256,384]{2,1,0:T(8,128)(2,1)S(1)}, bf16[1,256,384]{2,1,0:T(8,128)(2,1)}, u32[]{:S(2)}) copy-start(bf16[1,256,384]{2,1,0:T(8,128)(2,1)} %param.11) | copy-start | bytes 589828
  7.2 40.1 %copy-start.16 = (f32[128,8]{0,1:T(8,128)S(1)}, f32[128,8]{0,1:T(8,128)}, u32[]{:S(2)}) copy-start(f32[128,8]{0,1:T(8,128)} %param.10) | copy-start | bytes 12292
  7.2 40.3 %copy-start.14 = (bf16[128,256]{1,0:T(8,128)(2,1)S(1)}, bf16[128,256]{1,0:T(8,128)(2,1)}, u32[]{:S(2)}) copy-start(bf16[128,256]{1,0:T(8,128)(2,1)} %param.8) | copy-start | bytes 196612
  9.0 45.1 %all-to-all-start = ((s32[64,1,1]{2,1,0:T(1,128)}), s32[64,1,1]{2,1,0:T(1,128)S(1)}, u32[]{:S(2)}, u32[]{:S(2)}) async-start(s32[64,1,1]{2,1,0:T(1,128)} %copy.42), calls=%async_computation | async-start | bytes 65536 | tf_op jit(solution)/shard_map/all_to_all | solution.py:48
  47.4 6.7 %copy-start.12 = (f32[128,8]{1,0:T(8,128)}, f32[128,8]{1,0:T(8,128)S(1)}, u32[]{:S(2)}) copy-start(f32[128,8]{1,0:T(8,128)S(1)} %copy.40) | copy-start | bytes 12292
  47.5 21.7 %copy-start.15 = (bf16[128,256]{1,0:T(8,128)(2,1)S(1)}, bf16[128,256]{1,0:T(8,128)(2,1)}, u32[]{:S(2)}) copy-start(bf16[128,256]{1,0:T(8,128)(2,1)} %param.7) | copy-start | bytes 196612
  54.1 68.4 %all-to-all-start.3 = ((bf16[64,32,256]{2,1,0:T(8,128)(2,1)}), bf16[64,32,256]{2,1,0:T(8,128)(2,1)S(1)}, u32[]{:S(2)}, u32[]{:S(2)}) async-start(bf16[64,32,256]{2,1,0:T(8,128)(2,1)} %bitcast.17), calls=%async_computation.3 | async-start | bytes 2097152 | tf_op jit(solution)/shard_map/all_to_all | solution.py:78
  122.5 60.5 %all-to-all-start.1 = ((bf16[64,32,256]{2,1,0:T(8,128)(2,1)}), bf16[64,32,256]{2,1,0:T(8,128)(2,1)S(1)}, u32[]{:S(2)}, u32[]{:S(2)}) async-start(bf16[64,32,256]{2,1,0:T(8,128)(2,1)} %bitcast.7), calls=%async_computation.1 | async-start | bytes 2097152 | tf_op jit(solution)/shard_map/all_to_all | solution.py:47
  129.3 63.2 %copy-start.10 = (bf16[1,256,384]{2,1,0:T(8,128)(2,1)S(1)}, bf16[1,256,384]{2,1,0:T(8,128)(2,1)}, u32[]{:S(2)}) copy-start(bf16[1,256,384]{2,1,0:T(8,128)(2,1)} %param.12) | copy-start | bytes 589828
  129.3 146.1 %all-reduce.3.cloned.1.call-start = ((), (), s32[]{:S(2)}) async-start(), calls=%async_computation.5 | async-start | bytes 8257536 | tf_op jit(solution)/shard_map/psum | solution.py:70
  140.7 55.3 %copy-start.8 = (bf16[1792,256]{1,0:T(8,128)(2,1)}, bf16[1792,256]{1,0:T(8,128)(2,1)S(1)}, u32[]{:S(2)}) copy-start(bf16[1792,256]{1,0:T(8,128)(2,1)S(1)} %scatter_custom_fusion.3) | copy-start | bytes 2752516
  192.6 3.5 copy-start.1
  194.3 1.8 copy-start.11
  279.3 1.1 copy-start.3
  279.3 1.5 copy-start.5
  279.3 26.8 %copy-start.6 = (bf16[1792,384]{1,0:T(8,128)(2,1)}, bf16[1792,384]{1,0:T(8,128)(2,1)S(1)}, u32[]{:S(2)}) copy-start(bf16[1792,384]{1,0:T(8,128)(2,1)S(1)} %get-tuple-element.10) | copy-start | bytes 4128772
  290.4 67.0 %all-to-all-start.4 = ((bf16[64,32,256]{2,1,0:T(8,128)(2,1)}), bf16[64,32,256]{2,1,0:T(8,128)(2,1)S(1)}, u32[]{:S(2)}, u32[]{:S(2)}) async-start(bf16[64,32,256]{2,1,0:T(8,128)(2,1)} %bitcast.68), calls=%async_computation.4 | async-start | bytes 2097152 | tf_op jit(solution)/shard_map/all_to_all | solution.py:91
  316.6 51.4 %copy-start.2 = (bf16[1792,256]{1,0:T(8,128)(2,1)S(1)}, bf16[1792,256]{1,0:T(8,128)(2,1)}, u32[]{:S(2)}) copy-start(bf16[1792,256]{1,0:T(8,128)(2,1)} %copy-done.1) | copy-start | bytes 2752516
  357.4 64.8 %all-to-all-start.2 = ((bf16[64,32,256]{2,1,0:T(8,128)(2,1)}), bf16[64,32,256]{2,1,0:T(8,128)(2,1)S(1)}, u32[]{:S(2)}, u32[]{:S(2)}) async-start(bf16[64,32,256]{2,1,0:T(8,128)(2,1)} %bitcast.67), calls=%async_computation.2 | async-start | bytes 2097152 | tf_op jit(solution)/shard_map/all_to_all | solution.py:77
  368.0 2.9 copy-start.4
  370.9 1.4 copy-start.7
  370.9 1.6 copy-start.9
  422.3 3.9 copy-start.13
Sparse Core Ops, SparseCore 0:
  198.0 77.3 all-reduce.2
where the time goes:
time: 435 us; the launch traced here: 434 us
  waiting for transfers between devices  251 us (58%)
  starting transfers between devices  67.1 us (15%)
  local copies, waits for them, and re-layouts  54.5 us (13%)
  other arithmetic  33 us (8%)
  between operations  14.4 us (3%)
  matrix products  13.7 us (3%)
    psum x1, waiting for transfers between devices, shards(): lax.psum(up_part.astype(jnp.bfloat16), 'dp').astype(jnp.float32)  77.5 us
    all_to_all x1, waiting for transfers between devices, shards(): lax.all_to_all(grad_slots, 'expert', split_axis=0, concat_axis=0, tiled=T...  47.2 us
    all_to_all x1, waiting for transfers between devices, shards(): lax.all_to_all(unpack(expert_out), 'expert', split_axis=0, concat_axis=0,...  43.6 us
    all_to_all x1, waiting for transfers between devices, shards(): lax.all_to_all(x_slots, 'expert', split_axis=0, concat_axis=0, tiled=True)  42.3 us
    all_to_all x1, waiting for transfers between devices, shards(): lax.all_to_all(unpack(row_grad), 'expert', split_axis=0, concat_axis=0, t...  40.8 us
    scatter x2, local copies, waits for them, and re-layouts, pack_rows(): empty_rows.at[target]  19 us
    all_to_all x1, starting transfers between devices, shards(): lax.all_to_all(sent_counts, 'expert', split_axis=0, concat_axis=0, tiled=...  18.7 us
    another operation x4, other arithmetic  18.2 us
  transfers between devices with their start and end apart: 6, of which 5 were waited for; matrix products, arithmetic and copies ran while one was open for 15% of the time, Pallas kernels for 0%

commit v1 on v0

--- a/solution.py
+++ b/solution.py
@@ -1,7 +1,15 @@
+import functools
 import jax
 import jax.numpy as jnp
 from jax import lax
 from jax.sharding import PartitionSpec as P
+
+
+def _divide_zone(packet, ax_name):
+    return jnp.sum(lax.all_gather(packet, axis_name=ax_name), axis=0)
+
+
+series_lead = functools.partial(_divide_zone, ax_name="dp")
 
 
 def contract(left_side, right_side, left_dim, right_dim):
@@ -67,7 +75,7 @@
     up_part = jnp.dot(packed_x, up_matrix, preferred_element_type=jnp.float32)
     gate_in, up_in = (
         lax.psum(gate_part.astype(jnp.bfloat16), "dp").astype(jnp.float32),
-        lax.psum(up_part.astype(jnp.bfloat16), "dp").astype(jnp.float32),
+        series_lead(up_part.astype(jnp.bfloat16)).astype(jnp.float32),
     )
     activated, slope_silu = silu_parts(gate_in)
     hidden_act = (activated * up_in).astype(jnp.bfloat16)

time: 435 us -> 446 us (1.025)
  blocking collectives: 0 us -> 60.3 us
  waiting for transfers between devices: 251 us -> 203 us
  starting transfers between devices: 67.1 us -> 60.2 us
  other arithmetic: 33 us -> 38.3 us
    all_to_all x0 -> x1, blocking collectives: none -> 60.3 us  [shards(): lax.all_to_all(grad_slots, 'expert', split_axis=0, concat_axis=0, tiled=T...]
    all_to_all x1 -> x0, waiting for transfers between devices: 47.2 us -> none  [shards(): lax.all_to_all(grad_slots, 'expert', split_axis=0, concat_axis=0, tiled=T...]
    all_to_all x1 -> x0, starting transfers between devices: 15.1 us -> none  [shards(): lax.all_to_all(grad_slots, 'expert', split_axis=0, concat_axis=0, tiled=T...]
    psum x1, waiting for transfers between devices: 77.5 us -> 66.8 us  [shards(): lax.psum(gate_part.astype(jnp.bfloat16), 'dp').astype(jnp.float32)]
    all_to_all x1, waiting for transfers between devices: 42.3 us -> 51.6 us  [shards(): lax.all_to_all(x_slots, 'expert', split_axis=0, concat_axis=0, tiled=True)]
    all_to_all x1, starting transfers between devices: 6.81 us -> 15.3 us  [shards(): lax.all_to_all(x_slots, 'expert', split_axis=0, concat_axis=0, tiled=True)]
    reduce_sum x0 -> x1, other arithmetic: none -> 6.54 us  [_divide_zone(): return jnp.sum(lax.all_gather(packet, axis_name=ax_name), axis=0)]
  transfers between devices with their start and end apart: 6 -> 6, of which waited for: 5 -> 4; matrix products, arithmetic and copies ran while one was open for 15% -> 17% of each run, Pallas kernels for 0% -> 0%
where the time goes in v1:
time: 446 us; the launch traced here: 445 us
  waiting for transfers between devices  203 us (46%)
  blocking collectives  60.3 us (14%)
  starting transfers between devices  60.2 us (13%)
  local copies, waits for them, and re-layouts  55.3 us (12%)
  other arithmetic  38.3 us (9%)
  between operations  14.4 us (3%)
  matrix products  13.7 us (3%)
    psum x1, waiting for transfers between devices, shards(): lax.psum(gate_part.astype(jnp.bfloat16), 'dp').astype(jnp.float32)  66.8 us
    all_to_all x1, blocking collectives, shards(): lax.all_to_all(grad_slots, 'expert', split_axis=0, concat_axis=0, tiled=T...  60.3 us
    all_to_all x1, waiting for transfers between devices, shards(): lax.all_to_all(x_slots, 'expert', split_axis=0, concat_axis=0, tiled=True)  51.6 us
    all_to_all x1, waiting for transfers between devices, shards(): lax.all_to_all(unpack(expert_out), 'expert', split_axis=0, concat_axis=0,...  43.3 us
    all_to_all x1, waiting for transfers between devices, shards(): lax.all_to_all(unpack(row_grad), 'expert', split_axis=0, concat_axis=0, t...  41.3 us
    scatter x2, local copies, waits for them, and re-layouts, pack_rows(): empty_rows.at[target]  19.2 us
    all_to_all x1, starting transfers between devices, shards(): lax.all_to_all(sent_counts, 'expert', split_axis=0, concat_axis=0, tiled=...  18.7 us
    another operation x4, other arithmetic  18.2 us
  transfers between devices with their start and end apart: 6, of which 4 were waited for; matrix products, arithmetic and copies ran while one was open for 17% of the time, Pallas kernels for 0%

profile of v1, /device:TPU:6, one launch (start us, length us, event | category | flops | bytes accessed | tf_op | source)
XLA Modules:
  0.0 445.2 jit_solution(12896489023878251440)
XLA Ops:
  7.2 0.8 copy.41
  8.3 0.7 copy.42
  9.0 18.7 %all-to-all-start = ((s32[64,1,1]{2,1,0:T(1,128)}), s32[64,1,1]{2,1,0:T(1,128)S(1)}, u32[]{:S(2)}, u32[]{:S(2)}) async-start(s32[64,1,1]{2,1,0:T(1,128)} %copy.42), calls=%async_computation | async-start | bytes 65536 | tf_op jit(solution)/shard_map/all_to_all | solution.py:56
  28.7 18.0 %reduce-window.19 = s32[64,8,128]{2,1,0:T(8,128)S(1)} reduce-window(s32[64,8,128]{2,1,0:T(8,128)S(1)} %fusion.25, s32[]{:T(128)} %constant.9.clone.1), window={size=1x1x128 pad=0_0x0_0x127_0}, to_apply=%region_2.3 | reduce-window | flops 8323072 | bytes 524292 | tf_op jit(solution)/shard_map/reduce-window.1
  47.3 6.0 %scatter_custom_fusion = bf16[2048,256]{1,0:T(8,128)(2,1)} fusion(s32[1024]{0:T(1024)S(1)} %bitcast.78, bf16[]{:T(256)} %constant.8.clone.1, bf16[128,256]{1,0:T(8,128)(2,1)S(1)} %copy-done.15), kind=kCustom, calls=%fused_computation.38 | custom fusion | bytes 1114114 | tf_op jit(solution)/shard_map/scatter | solution.py:49
  53.4 15.3 %all-to-all-start.1 = ((bf16[64,32,256]{2,1,0:T(8,128)(2,1)}), bf16[64,32,256]{2,1,0:T(8,128)(2,1)S(1)}, u32[]{:S(2)}, u32[]{:S(2)}) async-start(bf16[64,32,256]{2,1,0:T(8,128)(2,1)} %bitcast.7), calls=%async_computation.1 | async-start | bytes 2097152 | tf_op jit(solution)/shard_map/all_to_all | solution.py:55
  68.9 1.2 reduce.3
  70.3 51.6 %all-to-all-done.1 = bf16[64,32,256]{2,1,0:T(8,128)(2,1)S(1)} async-done(((bf16[64,32,256]{2,1,0:T(8,128)(2,1)}), bf16[64,32,256]{2,1,0:T(8,128)(2,1)S(1)}, u32[]{:S(2)}, u32[]{:S(2)}) %all-to-all-start.1) | async-done | bytes 1048608 | tf_op jit(solution)/shard_map/all_to_all | solution.py:55
  121.9 9.5 %scatter_custom_fusion.1 = bf16[1792,256]{1,0:T(8,128)(2,1)S(1)} fusion(s32[2048]{0:T(1024)S(1)} %bitcast.81, bf16[2048,256]{1,0:T(8,128)(2,1)S(1)} %bitcast.72, bf16[]{:T(256)} %constant.8.clone.1), kind=kCustom, calls=%fused_computation.46 | custom fusion | bytes 917506 | tf_op jit(solution)/shard_map/scatter | solution.py:68
  131.4 1.7 convolution_convert_fusion.1
  134.2 5.7 %scatter_custom_fusion.2 = bf16[2048,256]{1,0:T(8,128)(2,1)S(1)} fusion(s32[1024]{0:T(1024)S(1)} %bitcast.79, f32[128,256]{1,0:T(8,128)S(1)} %convert_element_type.72, f32[1024]{0:T(1024)S(1)} %mul.74, bf16[]{:T(256)} %constant.8.clone.1), kind=kCustom, calls=%fused_computation.36 | custom fusion | flops 524288 | bytes 1183746 | tf_op jit(solution)/shard_map/scatter | solution.py:49
  139.9 60.3 %all_to_all.29 = bf16[64,32,256]{2,1,0:T(8,128)(2,1)S(1)} all-to-all(bf16[64,32,256]{2,1,0:T(8,128)(2,1)S(1)} %bitcast.69), channel_id=1, replica_groups=mesh['dp'=8,'expert'=64] {'expert'}, dimensions={0} | all-to-all | bytes 2097152 | tf_op jit(solution)/shard_map/all_to_all | solution.py:86
  200.3 9.7 %scatter_custom_fusion.3 = bf16[1792,256]{1,0:T(8,128)(2,1)S(1)} fusion(s32[2048]{0:T(1024)S(1)} %bitcast.82, bf16[2048,256]{1,0:T(8,128)(2,1)S(1)} %bitcast.73, bf16[]{:T(256)} %constant.8.clone.1), kind=kCustom, calls=%fused_computation.44 | custom fusion | bytes 917506 | tf_op jit(solution)/shard_map/scatter | solution.py:68
  210.0 1.7 convolution_convert_fusion.2
  211.8 1.7 convolution_convert_fusion
  213.6 6.5 %reduce_sum.56 = bf16[1792,384]{1,0:T(8,128)(2,1)S(1)} reduce(bf16[8,1792,384]{2,1,0:T(8,128)(2,1)} %bitcast.68, bf16[]{:T(256)} %constant.8.clone.1), dimensions={0}, to_apply=%region_8.9 | reduce | flops 4816896 | bytes 12386306 | tf_op jit(solution)/shard_map/reduce_sum | solution.py:9
  220.1 66.8 %all-reduce.3.cloned.1.call-done = (bf16[1792,384]{1,0:T(8,128)(2,1)}, bf16[1792,384]{1,0:T(8,128)(2,1)}) async-done(((bf16[1792,384]{1,0:T(8,128)(2,1)}, bf16[1792,384]{1,0:T(8,128)(2,1)}), (bf16[1792,384]{1,0:T(8,128)(2,1)}, bf16[1792,384]{1,0:T(8,128)(2,1)})) %all-reduce.3.cloned.1.call-update) | async-done | bytes 2752528 | tf_op jit(solution)/shard_map/psum | solution.py:77
  286.9 3.4 fusion.3
  292.6 9.0 %gather_fusion.2 = bf16[2048,256]{1,0:T(8,128)(2,1)} fusion(bf16[1792,256]{1,0:T(8,128)(2,1)S(1)} %fusion.9, s32[2048]{0:T(1024)S(1)} %broadcast_clamp_fusion), kind=kCustom, calls=%fused_computation.2 | custom fusion | bytes 2105344 | tf_op jit(solution)/shard_map/gather | solution.py:71
  301.5 15.6 %all-to-all-start.4 = ((bf16[64,32,256]{2,1,0:T(8,128)(2,1)}), bf16[64,32,256]{2,1,0:T(8,128)(2,1)S(1)}, u32[]{:S(2)}, u32[]{:S(2)}) async-start(bf16[64,32,256]{2,1,0:T(8,128)(2,1)} %bitcast.71), calls=%async_computation.4 | async-start | bytes 2097152 | tf_op jit(solution)/shard_map/all_to_all | solution.py:99
  317.2 1.6 convolution_convert_fusion.3
  318.8 9.0 %gather_fusion = bf16[2048,256]{1,0:T(8,128)(2,1)} fusion(bf16[1792,256]{1,0:T(8,128)(2,1)S(1)} %convolution_convert_fusion.3, s32[2048]{0:T(1024)S(1)} %broadcast_clamp_fusion), kind=kCustom, calls=%fused_computation | custom fusion | bytes 2105344 | tf_op jit(solution)/shard_map/gather | solution.py:71
  327.7 41.3 %all-to-all-done.4 = bf16[64,32,256]{2,1,0:T(8,128)(2,1)S(1)} async-done(((bf16[64,32,256]{2,1,0:T(8,128)(2,1)}), bf16[64,32,256]{2,1,0:T(8,128)(2,1)S(1)}, u32[]{:S(2)}, u32[]{:S(2)}) %all-to-all-start.4) | async-done | bytes 1048608 | tf_op jit(solution)/shard_map/all_to_all | solution.py:99
  369.0 10.3 %all-to-all-start.2 = ((bf16[64,32,256]{2,1,0:T(8,128)(2,1)}), bf16[64,32,256]{2,1,0:T(8,128)(2,1)S(1)}, u32[]{:S(2)}, u32[]{:S(2)}) async-start(bf16[64,32,256]{2,1,0:T(8,128)(2,1)} %bitcast.70), calls=%async_computation.2 | async-start | bytes 2097152 | tf_op jit(solution)/shard_map/all_to_all | solution.py:85
  379.4 2.9 convolution_bitcast_fusion.1
  382.3 1.4 convolution_bitcast_fusion.2
  383.9 1.3 convolution_bitcast_fusion
  385.2 3.9 gather_fusion.3
  389.1 1.0 bitcast_reduce_fusion
  390.1 43.3 %all-to-all-done.2 = bf16[64,32,256]{2,1,0:T(8,128)(2,1)S(1)} async-done(((bf16[64,32,256]{2,1,0:T(8,128)(2,1)}), bf16[64,32,256]{2,1,0:T(8,128)(2,1)S(1)}, u32[]{:S(2)}, u32[]{:S(2)}) %all-to-all-start.2) | async-done | bytes 1048608 | tf_op jit(solution)/shard_map/all_to_all | solution.py:85
  433.4 3.9 gather_fusion.1
  437.4 1.0 fusion.10
  (69 shorter events, 5.6 us)
Async XLA Ops:
  7.2 202.8 %copy-start = (bf16[1,256,384]{2,1,0:T(8,128)(2,1)S(1)}, bf16[1,256,384]{2,1,0:T(8,128)(2,1)}, u32[]{:S(2)}) copy-start(bf16[1,256,384]{2,1,0:T(8,128)(2,1)} %param.11) | copy-start | bytes 589828
  7.2 40.1 %copy-start.15 = (bf16[128,256]{1,0:T(8,128)(2,1)S(1)}, bf16[128,256]{1,0:T(8,128)(2,1)}, u32[]{:S(2)}) copy-start(bf16[128,256]{1,0:T(8,128)(2,1)} %param.7) | copy-start | bytes 196612
  9.0 44.4 %all-to-all-start = ((s32[64,1,1]{2,1,0:T(1,128)}), s32[64,1,1]{2,1,0:T(1,128)S(1)}, u32[]{:S(2)}, u32[]{:S(2)}) async-start(s32[64,1,1]{2,1,0:T(1,128)} %copy.42), calls=%async_computation | async-start | bytes 65536 | tf_op jit(solution)/shard_map/all_to_all | solution.py:56
  53.4 78.1 %copy-start.10 = (bf16[1,256,384]{2,1,0:T(8,128)(2,1)S(1)}, bf16[1,256,384]{2,1,0:T(8,128)(2,1)}, u32[]{:S(2)}) copy-start(bf16[1,256,384]{2,1,0:T(8,128)(2,1)} %param.12) | copy-start | bytes 589828
  53.4 68.5 %all-to-all-start.1 = ((bf16[64,32,256]{2,1,0:T(8,128)(2,1)}), bf16[64,32,256]{2,1,0:T(8,128)(2,1)S(1)}, u32[]{:S(2)}, u32[]{:S(2)}) async-start(bf16[64,32,256]{2,1,0:T(8,128)(2,1)} %bitcast.7), calls=%async_computation.1 | async-start | bytes 2097152 | tf_op jit(solution)/shard_map/all_to_all | solution.py:55
  68.6 145.0 %all-gather.3.cloned.1.call-start = ((), (), s32[]{:S(2)}) async-start(), calls=%async_computation.5 | async-start | bytes 12386304 | tf_op jit(solution)/shard_map/all_gather | solution.py:9
  131.4 78.6 %copy-start.1 = (bf16[1792,256]{1,0:T(8,128)(2,1)}, bf16[1792,256]{1,0:T(8,128)(2,1)S(1)}, u32[]{:S(2)}) copy-start(bf16[1792,256]{1,0:T(8,128)(2,1)S(1)} %scatter_custom_fusion.1) | copy-start | bytes 2752516
  131.4 2.0 copy-start.17
  133.2 1.0 copy-start.16
  133.2 153.7 %all-reduce.3.cloned.1.call-start = ((), (), s32[]{:S(2)}) async-start(), calls=%async_computation.6 | async-start | bytes 5505024 | tf_op jit(solution)/shard_map/psum | solution.py:77
  133.5 0.6 copy-start.13
  210.0 3.5 copy-start.8
  210.0 1.8 copy-start.12
  290.4 1.1 copy-start.3
  290.4 1.5 copy-start.5
  290.4 26.8 %copy-start.6 = (bf16[1792,384]{1,0:T(8,128)(2,1)}, bf16[1792,384]{1,0:T(8,128)(2,1)S(1)}, u32[]{:S(2)}) copy-start(bf16[1792,384]{1,0:T(8,128)(2,1)S(1)} %get-tuple-element.9) | copy-start | bytes 4128772
  290.4 1.5 copy-start.11
  301.5 67.5 %all-to-all-start.4 = ((bf16[64,32,256]{2,1,0:T(8,128)(2,1)}), bf16[64,32,256]{2,1,0:T(8,128)(2,1)S(1)}, u32[]{:S(2)}, u32[]{:S(2)}) async-start(bf16[64,32,256]{2,1,0:T(8,128)(2,1)} %bitcast.71), calls=%async_computation.4 | async-start | bytes 2097152 | tf_op jit(solution)/shard_map/all_to_all | solution.py:99
  327.7 51.7 %copy-start.2 = (bf16[1792,256]{1,0:T(8,128)(2,1)S(1)}, bf16[1792,256]{1,0:T(8,128)(2,1)}, u32[]{:S(2)}) copy-start(bf16[1792,256]{1,0:T(8,128)(2,1)} %copy-done.1) | copy-start | bytes 2752516
  369.0 64.4 %all-to-all-start.2 = ((bf16[64,32,256]{2,1,0:T(8,128)(2,1)}), bf16[64,32,256]{2,1,0:T(8,128)(2,1)S(1)}, u32[]{:S(2)}, u32[]{:S(2)}) async-start(bf16[64,32,256]{2,1,0:T(8,128)(2,1)} %bitcast.70), calls=%async_computation.2 | async-start | bytes 2097152 | tf_op jit(solution)/shard_map/all_to_all | solution.py:85
  379.4 2.9 copy-start.4
  382.3 1.4 copy-start.7
  382.3 1.6 copy-start.9
  433.4 3.9 copy-start.14
Sparse Core Ops, SparseCore 0:
  133.3 59.0 all-gather.2
  213.7 73.1 all-reduce.2
